TPU v7x, 256 devices: a whole 4x4x8 slice. The times are simulated.
256 devices in a mesh: sec: 16 (over z, core), term: 16 (over y, x).
Axes of the slice: x: 4, y: 4, z: 8, core: 2. Of those that a mesh axis runs over, the one named last changes fastest.
Arguments:
- psi: bfloat16 [16, 512, 512], P('sec'), may hold values from -6 to 6
- left_ops: bfloat16 [16, 96, 512, 512], P('sec', 'term'), may hold values from -0.078125 to 0.078125
- right_ops: bfloat16 [16, 96, 512, 512], P('sec', 'term'), may hold values from -0.078125 to 0.078125
- term_mask: int32 [16, 96], P('sec', 'term'), may hold values 0 or 1
- pair_src: int32 [16], P('sec'), may hold values from 0 to 15, each once
- pair_dst: int32 [16], P('sec'), may hold values from 0 to 15, each once
Outputs:
- sigma: bfloat16 [16, 512, 512], P('sec')
Inputs may be any that keep to these rules, and one draw needn't show every extreme that they name: `pair_src`: each of the 16 sector blocks is the source of exactly one pair. `pair_dst`: each of the 16 sector blocks is the target of exactly one pair.
All inputs are finite; a program needn't handle non-finite values. No bound on the sum of `term_mask` on one device may be relied on, other than what follows from the above.
Results may differ from a plain program's by a relative error of at most 0.0065.
Values may be sent and summed in bfloat16 or wider, within the bound.
A program may use at most 64 MiB of HBM per device.

v0:
```python
import jax
import jax.numpy as jnp
from jax import lax
from jax.sharding import PartitionSpec as P


def in_blocks(value, dim, peers):
    shape = value.shape
    pieces = value.reshape(*shape[:dim], peers, shape[dim] // peers, *shape[dim + 1 :])
    return jnp.moveaxis(pieces, dim, 0)


def sent_and_summed(value, axis, dim):
    pieces = in_blocks(value, dim, lax.axis_size(axis))
    arrived = lax.all_to_all(pieces, axis, split_axis=0, concat_axis=0, tiled=True)
    return arrived.astype(jnp.float32).sum(axis=0)


def in_one_piece(arrays, axis, dim, along):
    columns = [a.reshape(*a.shape[:along], -1) for a in arrays]
    both = jnp.concatenate(columns, axis=along)
    filled, at, finished = (lax.all_gather(both, axis, axis=dim, tiled=True), 0, [])
    for a, column in zip(arrays, columns):
        piece = filled[..., at : at + column.shape[along]]
        finished.append(piece.reshape(*piece.shape[:along], *a.shape[along:]))
        at += column.shape[along]
    return tuple(finished)


def in_order(pieces, dim):
    pieces = jnp.moveaxis(pieces, 0, dim)
    shape = pieces.shape
    return pieces.reshape(*shape[:dim], shape[dim] * shape[dim + 1], *shape[dim + 2 :])


def copy_for_each(value, axis):
    peers = lax.axis_size(axis)
    return lax.all_to_all(
        jnp.broadcast_to(value[None], (peers, *value.shape)), axis, 0, 0, tiled=True
    )


def gathered_copies(value, axis, dim):
    return in_order(copy_for_each(value, axis), dim)


def local(psi, left_ops, right_ops, term_mask, pair_src, pair_dst):
    whole = lax.all_gather(psi, "sec", axis=0, tiled=True)
    order = psi.shape[1]
    local_pairs = psi.shape[0]
    local_terms = left_ops.shape[1]
    zero_block = jnp.zeros((order, order), jnp.float32)
    source = pair_src[0]
    target = pair_dst[0]
    src_block = lax.dynamic_index_in_dim(whole, source, 0, keepdims=False)
    dst_block = lax.dynamic_index_in_dim(whole, target, 0, keepdims=False)

    def term_step(acc, term):

        def active(carry):
            fwd_acc, adj_acc = carry
            left = left_ops[0, term]
            right = right_ops[0, term]
            inner_fwd = jnp.dot(left, src_block, preferred_element_type=jnp.float32).astype(
                jnp.bfloat16
            )
            inner_adj = jnp.dot(left.T, dst_block, preferred_element_type=jnp.float32).astype(
                jnp.bfloat16
            )
            fwd_acc = fwd_acc + jnp.dot(inner_fwd, right.T, preferred_element_type=jnp.float32)
            adj_acc = adj_acc + jnp.dot(inner_adj, right, preferred_element_type=jnp.float32)
            return (fwd_acc, adj_acc)

        return (lax.cond(term_mask[0, term] == 1, active, lambda carry: carry, acc), None)

    (fwd, adj), _ = lax.scan(
        term_step, (zero_block, zero_block), jnp.arange(local_terms, dtype=jnp.int32)
    )
    fwd_list = [fwd]
    adj_list = [adj]
    stacked = jnp.stack([jnp.stack(fwd_list), jnp.stack(adj_list)], axis=1)
    pieces = sent_and_summed(stacked.astype(jnp.bfloat16), "term", 2)
    all_pieces, all_src, all_dst = in_one_piece(
        (pieces, pair_src.astype(jnp.float32), pair_dst.astype(jnp.float32)), "sec", 0, 1
    )
    mine = (lax.axis_index("sec") * local_pairs + jnp.arange(local_pairs, dtype=jnp.int32)).astype(
        jnp.float32
    )
    pick_fwd = (all_dst[None, :] == mine[:, None]).astype(jnp.float32)
    pick_adj = (all_src[None, :] == mine[:, None]).astype(jnp.float32)
    rows_fwd = jnp.einsum(
        "sk,krc->src", pick_fwd, all_pieces[:, 0], precision=lax.Precision.HIGHEST
    )
    rows_adj = jnp.einsum(
        "sk,krc->src", pick_adj, all_pieces[:, 1], precision=lax.Precision.HIGHEST
    )
    rows = (rows_fwd + rows_adj).astype(jnp.bfloat16)
    return gathered_copies(rows, "term", 1)


def solution(mesh):
    placed = (
        P("sec", None, None),
        P("sec", "term", None, None),
        P("sec", "term", None, None),
        P("sec", "term"),
        P("sec"),
        P("sec"),
    )
    return jax.shard_map(
        local, mesh=mesh, in_specs=placed, out_specs=P("sec", None, None), check_vma=False
    )
```

profile of v0, /device:TPU:1, one launch (start us, length us, event | category | flops | bytes accessed | tf_op | source)
XLA Modules:
  0.0 217.2 jit_solution(3146875595708951832)
XLA Ops:
  6.5 0.0 copy-start.1
  6.5 0.0 all-gather.4.cloned.1.call-start
  6.5 0.7 all-gather.4.cloned.1.call-update
  8.6 60.7 %all-gather.4.cloned.1.call-done = bf16[16,512,512]{2,1,0:T(8,128)(2,1)} async-done(((bf16[1,512,512]{2,1,0:T(8,128)(2,1)}), bf16[16,512,512]{2,1,0:T(8,128)(2,1)}) %all-gather.4.cloned.1.call-update) | async-done | bytes 8388624 | tf_op jit(solution)/shard_map/all_gather | solution.py:48
  69.2 1.3 dynamic-slice_bitcast_fusion
  70.5 0.1 broadcast_in_dim.4
  70.6 0.1 broadcast_in_dim.4.clone
  70.8 0.0 copy-done.1
  70.8 35.9 %while.12 = (s32[]{:T(128)}, f32[512,512]{1,0:T(8,128)S(1)}, f32[512,512]{1,0:T(8,128)S(1)}, s32[6]{0:T(128)S(1)}, s32[1,6]{1,0:T(1,128)S(1)}, /*index=5*/bf16[1...) while((s32[]{:T(128)}, f32[512,512]{1,0:T(8,128)S(1)}, ...), condition=%wide.region_3.4_spmd, body=%wide.region_0.3_spmd.sunk | while | flops 1074790400 | bytes 7342387 | solution.py:76
  70.8 0.7 dynamic_slice.44
  73.5 0.6 fusion.29
  74.7 6.0 %conditional.2 = ((f32[512,512]{1,0:T(8,128)S(1)}, f32[512,512]{1,0:T(8,128)S(1)})) conditional(s32[]{:T(128)} %bitcast.55, (f32[512,512]{1,0:T(8,128)S(1)}, f32[512,512]{1,0:T(8,128)S(1)}) %tuple.30, (s32[]{:T(128)}, bf16[1,6,512,512]{3,2,1,0:T(8,128)(2,1)}, bf16[512,512]{1,0:T(8,128)(2,1)S(1)}, bf16[1,6,512,512]{3,2,1,0:T(8,128)(2,1)}, ...), branch_computations={%region_1.1_spmd, %region_2.2_spmd} | conditional | flops 1074790400 | bytes 7342138 | solution.py:74
  76.8 1.9 convolution_add_fusion
  78.8 1.9 convolution_add_fusion.1
  80.7 0.7 dynamic_slice.44
  83.4 0.6 fusion.29
  84.7 0.7 dynamic_slice.44
  87.4 0.6 fusion.29
  88.7 0.7 dynamic_slice.44
  91.4 0.6 fusion.29
  92.7 6.0 %conditional.2 = ((f32[512,512]{1,0:T(8,128)S(1)}, f32[512,512]{1,0:T(8,128)S(1)})) conditional(s32[]{:T(128)} %bitcast.55, (f32[512,512]{1,0:T(8,128)S(1)}, f32[512,512]{1,0:T(8,128)S(1)}) %tuple.30, (s32[]{:T(128)}, bf16[1,6,512,512]{3,2,1,0:T(8,128)(2,1)}, bf16[512,512]{1,0:T(8,128)(2,1)S(1)}, bf16[1,6,512,512]{3,2,1,0:T(8,128)(2,1)}, ...), branch_computations={%region_1.1_spmd, %region_2.2_spmd} | conditional | flops 1074790400 | bytes 7342138 | solution.py:74
  94.7 1.9 convolution_add_fusion
  96.7 1.9 convolution_add_fusion.1
  98.7 0.7 dynamic_slice.44
  101.4 0.6 fusion.29
  102.7 0.7 dynamic_slice.44
  105.4 0.6 fusion.29
  106.6 0.1 convert.9
  106.7 0.1 convert.10
  106.8 1.1 maximum_bitcast_fusion
  107.9 24.4 %all-to-all-start = ((bf16[16,1,2,32,512]{4,3,2,1,0:T(8,128)(2,1)}), bf16[16,1,2,32,512]{4,3,2,1,0:T(8,128)(2,1)S(1)}, u32[]{:S(2)}, u32[]{:S(2)}) async-start(bf16[16,1,2,32,512]{4,3,2,1,0:T(8,128)(2,1)} %maximum_bitcast_fusion), calls=%async_computation | async-start | bytes 2097152 | tf_op jit(solution)/shard_map/all_to_all | solution.py:15
  132.2 0.0 all-gather.6.cloned.1.call-start
  132.3 16.5 %all-to-all-done = bf16[16,1,2,32,512]{4,3,2,1,0:T(8,128)(2,1)S(1)} async-done(((bf16[16,1,2,32,512]{4,3,2,1,0:T(8,128)(2,1)}), bf16[16,1,2,32,512]{4,3,2,1,0:T(8,128)(2,1)S(1)}, u32[]{:S(2)}, u32[]{:S(2)}) %all-to-all-start) | async-done | bytes 1048608 | tf_op jit(solution)/shard_map/all_to_all | solution.py:15
  148.8 0.1 convert_reduce_fusion
  148.9 0.1 reshape.86
  149.1 0.1 dynamic-update-slice.2
  149.3 0.7 copy-done
  149.9 0.0 all-gather.6.cloned.1.call-update
  149.9 36.7 %all-gather.6.cloned.1.call-done = f32[16,1,32770]{2,1,0:T(1,128)} async-done(((f32[1,1,32770]{2,1,0:T(1,128)}), f32[16,1,32770]{2,1,0:T(1,128)}) %all-gather.6.cloned.1.call-update) | async-done | bytes 2097296 | tf_op jit(solution)/shard_map/all_gather | solution.py:22
  186.6 1.7 copy.20
  188.3 0.1 slice.21
  188.5 1.2 copy.12
  189.7 0.3 slice_bitcast_fusion.1
  190.0 0.2 fusion.21
  190.2 1.1 fusion.18
  191.3 1.1 fusion.16
  192.4 17.1 %all_to_all.10 = bf16[16,1,32,512]{3,2,1,0:T(8,128)(2,1)S(1)} all-to-all(bf16[16,1,32,512]{3,2,1,0:T(8,128)(2,1)S(1)} %broadcast_in_dim.5), channel_id=1, replica_groups=mesh['sec'=16,'term'=16] {'term'}, dimensions={0} | all-to-all | bytes 1048576 | tf_op jit(solution)/shard_map/all_to_all | solution.py:38
  209.6 0.8 copy.39
  (10 shorter events, 0.2 us)
Async XLA Ops:
  6.5 64.2 %copy-start.1 = (s32[1,6]{1,0:T(1,128)S(1)}, s32[1,6]{1,0:T(1,128)}, u32[]{:S(2)}) copy-start(s32[1,6]{1,0:T(1,128)} %param.13) | copy-start | bytes 76
  6.5 62.7 %all-gather.4.cloned.1.call-start = ((), (), s32[]{:S(2)}) async-start(), calls=%async_computation.2 | async-start | bytes 8912896 | tf_op jit(solution)/shard_map/all_gather | solution.py:48
  107.9 40.9 %all-to-all-start = ((bf16[16,1,2,32,512]{4,3,2,1,0:T(8,128)(2,1)}), bf16[16,1,2,32,512]{4,3,2,1,0:T(8,128)(2,1)S(1)}, u32[]{:S(2)}, u32[]{:S(2)}) async-start(bf16[16,1,2,32,512]{4,3,2,1,0:T(8,128)(2,1)} %maximum_bitcast_fusion), calls=%async_computation | async-start | bytes 2097152 | tf_op jit(solution)/shard_map/all_to_all | solution.py:15
  132.2 54.4 %all-gather.6.cloned.1.call-start = ((), (), s32[]{:S(2)}) async-start(), calls=%async_computation.3 | async-start | bytes 2236928 | tf_op jit(solution)/shard_map/all_gather | solution.py:22
  149.3 0.7 copy-start
Sparse Core Ops, SparseCore 0:
  9.2 60.0 all-gather.3
  150.1 36.4 all-gather.5
where the time goes:
time: 218 us; the launch traced here: 217 us
  waiting for transfers between devices  115 us (53%)
  starting transfers between devices  24.4 us (11%)
  loops' own time  20.5 us (9%)
  blocking collectives  17.1 us (8%)
  between operations  14.9 us (7%)
  local copies, waits for them, and re-layouts  10.6 us (5%)
  matrix products  9.94 us (5%)
  other arithmetic  5.21 us (2%)
    all_gather x1, waiting for transfers between devices, local(): whole = lax.all_gather(psi, 'sec', axis=0, tiled=True)  60.7 us
    all_gather x1, waiting for transfers between devices, in_one_piece(): lax.all_gather(both, axis, axis=dim, tiled=True)  36.7 us
    all_to_all x1, starting transfers between devices, sent_and_summed(): lax.all_to_all(pieces, axis, split_axis=0, concat_axis=0, tiled=True)  24.4 us
    all_to_all x1, blocking collectives, copy_for_each(): lax.all_to_all(jnp.broadcast_to(value[None], (peers, *value.shape)), axis...  17.1 us
    all_to_all x1, waiting for transfers between devices, sent_and_summed(): lax.all_to_all(pieces, axis, split_axis=0, concat_axis=0, tiled=True)  16.5 us
    another operation x1, loops' own time, local(): lax.scan(term_step, (zero_block, zero_block), jnp.arange(local_terms, dty...  16.3 us
    unnamed x9, local copies, waits for them, and re-layouts  4.47 us
  transfers between devices with their start and end apart: 3, of which 3 were waited for; matrix products, arithmetic and copies ran while one was open for 0% of the time, Pallas kernels for 0%

commit v1 on v0

v1 whole, which is shorter than its diff:
```python
import functools

import jax
import jax.numpy as jnp
from jax import lax
from jax.experimental import pallas as pl
from jax.experimental.pallas import tpu as pltpu
from jax.sharding import PartitionSpec as P

MESH = pl.DeviceIdType.MESH
F32, BF16 = jnp.float32, jnp.bfloat16


def remote(src, dst, send_sem, recv_sem, device):
    return pltpu.make_async_remote_copy(
        src_ref=src,
        dst_ref=dst,
        send_sem=send_sem,
        recv_sem=recv_sem,
        device_id=device,
        device_id_type=MESH,
    )


def wait_for(ref, sem):
    pltpu.make_async_copy(ref, ref, sem).wait()


def kernel(
    sizes,
    psi,
    left,
    right,
    mask,
    src,
    dst,
    out,
    left_v,
    right_v,
    column,
    handed,
    given,
    blocks,
    label,
    labels,
    label_p,
    total,
    part,
    arrived,
    rows_out,
    rows_in,
    mine_v,
    local_sem,
    send_sem,
    recv_sem,
):
    nsec, nterm, terms, order = sizes
    nz = nsec // 2
    rows = order // nterm
    s, t = lax.axis_index("sec"), lax.axis_index("term")
    z, c = s // 2, s % 2
    partner = {"sec": z * 2 + (1 - c)}

    def on_z(d):
        return {"sec": ((z + nz - d) % nz) * 2 + c}

    def on_term(j):
        return {"term": (t + j) % nterm}

    def row_block(index):
        return pl.ds(pl.multiple_of(index * rows, rows), rows)

    far_first = sorted(range(1, nz), key=lambda d: -min(d, nz - d))

    load_left = pltpu.make_async_copy(left.at[0], left_v, local_sem.at[0])
    load_right = pltpu.make_async_copy(right.at[0], right_v, local_sem.at[1])
    own = pltpu.make_async_copy(psi.at[0, row_block(t)], column.at[0], local_sem.at[2])
    own.start()

    label[0:8, :] = jnp.full((8, 128), src[0], jnp.int32).astype(F32)
    label[8:16, :] = jnp.full((8, 128), dst[0], jnp.int32).astype(F32)

    barrier = pltpu.get_barrier_semaphore()
    pl.semaphore_signal(barrier, inc=1, device_id=partner, device_id_type=MESH)
    for d in far_first:
        pl.semaphore_signal(barrier, inc=1, device_id=on_z(d), device_id_type=MESH)

    def greet(j, carry):
        pl.semaphore_signal(barrier, inc=1, device_id=on_term(j), device_id_type=MESH)
        return carry

    lax.fori_loop(1, nterm, greet, 0)
    pl.semaphore_wait(barrier, nz + nterm - 1)

    for d in far_first:
        remote(
            psi.at[0, row_block(t)], column.at[d], send_sem.at[0], recv_sem.at[0], on_z(d)
        ).start()
    remote(label, label_p, send_sem.at[1], recv_sem.at[1], partner).start()
    for d in far_first:
        remote(label, labels.at[d], send_sem.at[2], recv_sem.at[2], on_z(d)).start()
    load_left.start()
    load_right.start()

    def row_of(labels_row):
        return jnp.concatenate([labels_row] * (order // 128), axis=1)

    def owner(d):
        return (((z + d) % nz) * 2 + c).astype(F32)

    wait_for(label_p, recv_sem.at[1])
    own.wait()
    wait_for(column.at[pl.ds(1, nz - 1)], recv_sem.at[0])
    for which in range(2):
        wanted = row_of(label_p[8 * which : 8 * which + 1, :])

        def pick(d, value):
            return jnp.where(wanted == owner(d), column[d].astype(F32), value)

        value = jnp.zeros((rows, order), F32)
        for d in range(nz):
            value = pick(d, value)
        given[which] = value.astype(BF16)
        remote(
            given.at[which], handed.at[which], send_sem.at[3], recv_sem.at[3 + which], partner
        ).start()
    for which in range(2):
        wanted = (src, dst)[which][0]
        local = column[(wanted // 2 + nz - z) % nz]
        wait_for(handed.at[which], recv_sem.at[3 + which])
        blocks[which, row_block(t), :] = jnp.where(wanted % 2 == c, local, handed[which])

        def send(j, carry):
            remote(
                blocks.at[which, row_block(t)],
                blocks.at[which, row_block(t)],
                send_sem.at[5 + which],
                recv_sem.at[5 + which],
                on_term(j),
            ).start()
            return carry

        lax.fori_loop(1, nterm, send, 0)

    others = pl.ds(0, (nterm - 1) * rows)
    load_left.wait()
    load_right.wait()
    for which in range(2):
        wait_for(blocks.at[which, others], recv_sem.at[5 + which])
        total[which] = jnp.zeros((order, order), F32)

        def add_term(term, carry):
            active = jnp.where(mask[0, term] == 1, 1.0, 0.0).astype(F32)
            if which == 0:
                inner = jnp.dot(left_v[term], blocks[which], preferred_element_type=F32)
                outer_dims = (((1,), (1,)), ((), ()))
            else:
                inner = lax.dot_general(
                    left_v[term],
                    blocks[which],
                    (((0,), (0,)), ((), ())),
                    preferred_element_type=F32,
                )
                outer_dims = (((1,), (0,)), ((), ()))
            inner = (inner * active).astype(BF16)
            total[which] += lax.dot_general(
                inner, right_v[term], outer_dims, preferred_element_type=F32
            )
            return carry

        lax.fori_loop(0, terms, add_term, 0)
        part[which] = total[which].astype(BF16)

        def scatter(j, carry):
            remote(
                part.at[which, row_block((t + j) % nterm)],
                arrived.at[which, nterm - 1 - j],
                send_sem.at[7 + which],
                recv_sem.at[7 + which],
                on_term(j),
            ).start()
            return carry

        lax.fori_loop(1, nterm, scatter, 0)

    for which in range(2):
        wait_for(arrived.at[which, pl.ds(0, nterm - 1)], recv_sem.at[7 + which])
        summed = total[which, row_block(t), :]
        for j in range(nterm - 1):
            summed = summed + arrived[which, j].astype(F32)
        rows_out[which] = summed.astype(BF16)
        for d in far_first:
            remote(
                rows_out.at[which],
                rows_in.at[which, d],
                send_sem.at[9 + which],
                recv_sem.at[9 + which],
                on_z(d),
            ).start()

    wait_for(labels.at[pl.ds(1, nz - 1)], recv_sem.at[2])
    for which in range(2):
        wait_for(rows_in.at[which, pl.ds(1, nz - 1)], recv_sem.at[9 + which])

    def collected(sector):
        sector = sector.astype(F32)
        value = jnp.zeros((rows, order), F32)
        for d in range(nz):
            tags = label if d == 0 else labels.at[d]
            for which in range(2):
                tag = row_of(tags[8 * (1 - which) : 8 * (1 - which) + 1, :])
                rows_d = rows_out[which] if d == 0 else rows_in[which, d]
                value = value + jnp.where(tag == sector, rows_d.astype(F32), 0.0)
        return value

    given[2] = collected(z * 2 + (1 - c)).astype(BF16)
    remote(given.at[2], handed.at[2], send_sem.at[11], recv_sem.at[11], partner).start()
    value = collected(s)
    wait_for(handed.at[2], recv_sem.at[11])
    mine_v[...] = (value + handed[2].astype(F32)).astype(BF16)
    keep = pltpu.make_async_copy(mine_v, out.at[0, row_block(t)], local_sem.at[2])
    keep.start()

    def spread(j, carry):
        remote(
            mine_v, out.at[0, row_block(t)], send_sem.at[12], recv_sem.at[12], on_term(j)
        ).start()
        return carry

    lax.fori_loop(1, nterm, spread, 0)

    wait_for(column.at[pl.ds(1, nz - 1)], send_sem.at[0])
    wait_for(label, send_sem.at[1])
    wait_for(labels.at[pl.ds(1, nz - 1)], send_sem.at[2])
    wait_for(given.at[pl.ds(0, 2)], send_sem.at[3])
    for which in range(2):
        wait_for(blocks.at[which, others], send_sem.at[5 + which])
        wait_for(part.at[which, others], send_sem.at[7 + which])
        wait_for(rows_in.at[which, pl.ds(1, nz - 1)], send_sem.at[9 + which])
    wait_for(given.at[2], send_sem.at[11])
    keep.wait()
    wait_for(out.at[0, others], send_sem.at[12])
    wait_for(out.at[0, others], recv_sem.at[12])


def solution(mesh):
    nsec, nterm = mesh.shape["sec"], mesh.shape["term"]
    placed = (
        P("sec", None, None),
        P("sec", "term", None, None),
        P("sec", "term", None, None),
        P("sec", "term"),
        P("sec"),
        P("sec"),
    )

    def local(psi, left_ops, right_ops, term_mask, pair_src, pair_dst):
        order, terms = psi.shape[1], left_ops.shape[1]
        rows, nz = order // nterm, nsec // 2
        anywhere = pl.BlockSpec(memory_space=pl.ANY)
        scalars = pl.BlockSpec(memory_space=pltpu.SMEM)
        return pl.pallas_call(
            functools.partial(kernel, (nsec, nterm, terms, order)),
            out_shape=jax.ShapeDtypeStruct(psi.shape, BF16),
            in_specs=[anywhere] * 3 + [scalars] * 3,
            out_specs=anywhere,
            scratch_shapes=[
                pltpu.VMEM((terms, order, order), BF16),
                pltpu.VMEM((terms, order, order), BF16),
                pltpu.VMEM((nz, rows, order), BF16),
                pltpu.VMEM((3, rows, order), BF16),
                pltpu.VMEM((3, rows, order), BF16),
                pltpu.VMEM((2, order, order), BF16),
                pltpu.VMEM((16, 128), F32),
                pltpu.VMEM((nz, 16, 128), F32),
                pltpu.VMEM((16, 128), F32),
                pltpu.VMEM((2, order, order), F32),
                pltpu.VMEM((2, order, order), BF16),
                pltpu.VMEM((2, nterm, rows, order), BF16),
                pltpu.VMEM((2, rows, order), BF16),
                pltpu.VMEM((2, nz, rows, order), BF16),
                pltpu.VMEM((rows, order), BF16),
                pltpu.SemaphoreType.DMA((3,)),
                pltpu.SemaphoreType.DMA((13,)),
                pltpu.SemaphoreType.DMA((13,)),
            ],
            compiler_params=pltpu.CompilerParams(
                collective_id=0, has_side_effects=True, vmem_limit_bytes=48 * 1024 * 1024
            ),
        )(psi, left_ops, right_ops, term_mask, pair_src, pair_dst)

    return jax.shard_map(
        local, mesh=mesh, in_specs=placed, out_specs=P("sec", None, None), check_vma=False
    )
```

time: 218 us -> 72.6 us (0.33)
  waiting for transfers between devices: 115 us -> 0 us
  Pallas kernels: 0 us -> 66.7 us
  starting transfers between devices: 24.4 us -> 0 us
  loops' own time: 20.5 us -> 0 us
  blocking collectives: 17.1 us -> 0 us
  between operations: 14.9 us -> 1.32 us
  matrix products: 9.94 us -> 0 us
  local copies, waits for them, and re-layouts: 10.6 us -> 4.37 us
  other arithmetic: 5.21 us -> 0 us
    all_gather x2 -> x0, waiting for transfers between devices: 97.3 us -> none  [the longest x1 60.7 us: local(): whole = lax.all_gather(psi, 'sec', axis=0, tiled=True)]
    pallas_call x0 -> x1, Pallas kernels: none -> 66.7 us  [local(): pl.pallas_call(functools.partial(kernel, (nsec, nterm, terms, order)), ou...]
    all_to_all x1 -> x0, starting transfers between devices: 24.4 us -> none  [sent_and_summed(): lax.all_to_all(pieces, axis, split_axis=0, concat_axis=0, tiled=True)]
    another operation x7 -> x0, loops' own time: 20.5 us -> none  [the longest x1 16.3 us: local(): lax.scan(term_step, (zero_block, zero_block), jnp.arange(local_terms, dty...]
    all_to_all x1 -> x0, blocking collectives: 17.1 us -> none  [copy_for_each(): lax.all_to_all(jnp.broadcast_to(value[None], (peers, *value.shape)), axis...]
    all_to_all x1 -> x0, waiting for transfers between devices: 16.5 us -> none  [sent_and_summed(): lax.all_to_all(pieces, axis, split_axis=0, concat_axis=0, tiled=True)]
    dot_general x6 -> x0, matrix products: 9.94 us -> none  [the longest x2 3.89 us: active(): jnp.dot(inner_adj, right, preferred_element_type=jnp.float32)]
    dynamic_slice x6 -> x0, local copies, waits for them, and re-layouts: 3.93 us -> none  [local(): lax.scan(term_step, (zero_block, zero_block), jnp.arange(local_terms, dty...]
  transfers between devices with their start and end apart: 3 -> 0, of which waited for: 3 -> 0; matrix products, arithmetic and copies ran while one was open for 0% -> 0% of each run, Pallas kernels for 0% -> 0%
where the time goes in v1:
time: 72.6 us; the launch traced here: 72.4 us
  Pallas kernels  66.7 us (92%)
  local copies, waits for them, and re-layouts  4.37 us (6%)
  between operations  1.32 us (2%)
    pallas_call x1, Pallas kernels, local(): pl.pallas_call(functools.partial(kernel, (nsec, nterm, terms, order)), ou...  66.7 us
    unnamed x7, local copies, waits for them, and re-layouts  4.37 us

profile of v1, /device:TPU:1, one launch (start us, length us, event | category | flops | bytes accessed | tf_op | source)
XLA Modules:
  0.0 72.4 jit_solution(3687485228364175806)
XLA Ops:
  1.3 0.0 copy-start
  1.3 1.9 %copy-done = bf16[1,6,512,512]{3,2,1,0:T(8,128)(2,1)S(1)} copy-done((bf16[1,6,512,512]{3,2,1,0:T(8,128)(2,1)S(1)}, bf16[1,6,512,512]{3,2,1,0:T(8,128)(2,1)}, u32[]{:S(2)}) %copy-start) | copy-done | bytes 3145752
  3.2 0.0 copy-start.1
  3.2 1.0 %copy-done.1 = bf16[1,512,512]{2,1,0:T(8,128)(2,1)S(1)} copy-done((bf16[1,512,512]{2,1,0:T(8,128)(2,1)S(1)}, bf16[1,512,512]{2,1,0:T(8,128)(2,1)}, u32[]{:S(2)}) %copy-start.1) | copy-done | bytes 524312
  4.2 0.0 copy-start.2
  4.2 0.7 copy-done.2
  4.9 66.7 %shard_map.64 = bf16[1,512,512]{2,1,0:T(8,128)(2,1)S(1)} custom-call(bf16[1,512,512]{2,1,0:T(8,128)(2,1)S(1)} %copy-done.1, bf16[1,6,512,512]{3,2,1,0:T(8,128)(2,1)S(1)} %copy-done, bf16[1,6,512,512]{3,2,1,0:T(8,128)(2,1)} %right.1, s32[1,6]{1,0:T(1,128)S(1)} %copy-done.2, s32[1]{0:T(128)S(6)} %copy.8.src, s32[1]{0:T(128)S(6)} %copy.9.dst), custom_call_target="tpu_custom_call" | custom-call | tf_op jit(solution)/shard_map/pallas_call | solution.py:262
  71.6 0.8 %copy.10 = bf16[1,512,512]{2,1,0:T(8,128)(2,1)} copy(bf16[1,512,512]{2,1,0:T(8,128)(2,1)S(1)} %shard_map.64) | data formatting | bytes 1048576
Async XLA Ops:
  1.3 1.9 %copy-start = (bf16[1,6,512,512]{3,2,1,0:T(8,128)(2,1)S(1)}, bf16[1,6,512,512]{3,2,1,0:T(8,128)(2,1)}, u32[]{:S(2)}) copy-start(bf16[1,6,512,512]{3,2,1,0:T(8,128)(2,1)} %left.1) | copy-start | bytes 9437188
  3.2 1.0 %copy-start.1 = (bf16[1,512,512]{2,1,0:T(8,128)(2,1)S(1)}, bf16[1,512,512]{2,1,0:T(8,128)(2,1)}, u32[]{:S(2)}) copy-start(bf16[1,512,512]{2,1,0:T(8,128)(2,1)} %psi.1) | copy-start | bytes 1572868
  4.2 0.7 copy-start.2

commit v2 on v1

v2 whole, which is shorter than its diff:
```python
import functools

import jax
import jax.numpy as jnp
from jax import lax
from jax.experimental import pallas as pl
from jax.experimental.pallas import tpu as pltpu
from jax.sharding import PartitionSpec as P

MESH = pl.DeviceIdType.MESH
F32, BF16 = jnp.float32, jnp.bfloat16


def remote(src, dst, send_sem, recv_sem, device):
    return pltpu.make_async_remote_copy(
        src_ref=src,
        dst_ref=dst,
        send_sem=send_sem,
        recv_sem=recv_sem,
        device_id=device,
        device_id_type=MESH,
    )


def wait_for(ref, sem):
    pltpu.make_async_copy(ref, ref, sem).wait()


def kernel(
    sizes,
    psi,
    left,
    right,
    mask,
    src,
    dst,
    out,
    left_v,
    right_v,
    column_a,
    column_b,
    handed,
    given,
    blocks,
    label,
    label_p,
    inner_v,
    total,
    part,
    arrived,
    sums,
    sums_p,
    leaving,
    landed,
    mine_v,
    mask_s,
    src_s,
    dst_s,
    local_sem,
    hand_send,
    hand_recv,
    column_send,
    column_recv,
    block_send,
    block_recv,
    part_send,
    part_recv,
    swap_send,
    swap_recv,
    land_send,
    land_recv,
    out_send,
    out_recv,
):
    nsec, nterm, terms, order = sizes
    column = (column_a, column_b)
    nz = nsec // 2
    rows = order // nterm
    wide = order // 2
    s, t = lax.axis_index("sec"), lax.axis_index("term")
    z, c = s // 2, s % 2
    partner = {"sec": z * 2 + (1 - c)}
    halves = [pl.ds(h * wide, wide) for h in range(2)]
    other_z = pl.ds(1, nz - 1)
    other_t = pl.ds(0, nterm - 1)
    other_rows = pl.ds(0, (nterm - 1) * rows)

    def on_z(d):
        return {"sec": ((z + nz - d) % nz) * 2 + c}

    def on_term(j):
        return {"term": (t + j) % nterm}

    def row_block(index):
        return pl.ds(pl.multiple_of(index * rows, rows), rows)

    def to_all_terms(make):
        def start(j, carry):
            make(j).start()
            return carry

        lax.fori_loop(1, nterm, start, 0)

    my_rows = row_block(t)
    far_first = sorted(range(1, nz), key=lambda d: -min(d, nz - d))

    scalars = [
        pltpu.make_async_copy(a, b, local_sem.at[3 + i])
        for i, (a, b) in enumerate(((mask, mask_s), (src, src_s), (dst, dst_s)))
    ]
    for copy in scalars:
        copy.start()
    own = [
        pltpu.make_async_copy(psi.at[0, my_rows, halves[h]], column[h].at[0], local_sem.at[1 + h])
        for h in range(2)
    ]
    for copy in own:
        copy.start()

    barrier = pltpu.get_barrier_semaphore()
    for d in far_first:
        pl.semaphore_signal(barrier, inc=1, device_id=on_z(d), device_id_type=MESH)
    pl.semaphore_signal(barrier, inc=1, device_id=partner, device_id_type=MESH)

    def greet(j, carry):
        pl.semaphore_signal(barrier, inc=1, device_id=on_term(j), device_id_type=MESH)
        return carry

    lax.fori_loop(1, nterm, greet, 0)
    for copy in scalars:
        copy.wait()
    ends = (src_s[0], dst_s[0])
    for which in range(2):
        label[8 * which : 8 * which + 8, :] = jnp.full((8, 128), ends[which], jnp.int32).astype(F32)
    for copy in own:
        copy.wait()
    pl.semaphore_wait(barrier, nz + nterm - 1)

    remote(label, label_p, hand_send.at[4], hand_recv.at[4], partner).start()
    for h in range(2):
        for d in far_first:
            remote(
                column[h].at[0],
                column[h].at[d],
                column_send.at[h],
                column_recv.at[h],
                on_z(d),
            ).start()
    load_left = pltpu.make_async_copy(left.at[0], left_v, local_sem.at[0])
    load_right = pltpu.make_async_copy(right.at[0], right_v, local_sem.at[1])
    load_left.start()
    load_right.start()

    def tag_row(which):
        row = label_p[8 * which : 8 * which + 1, :]
        return jnp.concatenate([row] * (wide // 128), axis=1)

    wait_for(label_p, hand_recv.at[4])

    def give(h):
        wait_for(column[h].at[other_z], column_recv.at[h])
        for which in range(2):
            wanted = tag_row(which)
            value = jnp.zeros((rows, wide), F32)
            for d in range(nz):
                here = (((z + d) % nz) * 2 + c).astype(F32)
                value = jnp.where(wanted == here, column[h][d].astype(F32), value)
            given[which, :, halves[h]] = value.astype(BF16)
            sem = 2 * which + h
            remote(
                given.at[which, :, halves[h]],
                handed.at[which, :, halves[h]],
                hand_send.at[sem],
                hand_recv.at[sem],
                partner,
            ).start()

    def place(which, h):
        wait_for(handed.at[which, :, halves[h]], hand_recv.at[2 * which + h])
        wanted = ends[which]
        local = column[h][(wanted // 2 + nz - z) % nz]
        blocks[which, my_rows, halves[h]] = jnp.where(
            wanted % 2 == c, local, handed[which, :, halves[h]]
        )
        to_all_terms(
            lambda j: remote(
                blocks.at[which, my_rows, halves[h]],
                blocks.at[which, my_rows, halves[h]],
                block_send.at[which, h],
                block_recv.at[which, h],
                on_term(j),
            )
        )

    give(0)
    place(0, 0)
    give(1)
    place(0, 1)
    place(1, 0)
    place(1, 1)

    def inner(which):
        for h in range(2):
            wait_for(blocks.at[which, other_rows, halves[h]], block_recv.at[which, h])

        def one(term, carry):
            active = jnp.where(mask_s[0, term] == 1, 1.0, 0.0).astype(F32)
            value = lax.dot_general(
                left_v[term],
                blocks[which],
                (((1 - which,), (0,)), ((), ())),
                preferred_element_type=F32,
            )
            inner_v[term] = (value * active).astype(BF16)
            return carry

        lax.fori_loop(0, terms, one, 0)

    def outer(which, h):
        value = jnp.zeros((order, wide), F32)
        for term in range(terms):
            operator = right_v[term, :, halves[h]] if which else right_v[term, halves[h], :]
            value = value + lax.dot_general(
                inner_v[term],
                operator,
                (((1,), (1 - which,)), ((), ())),
                preferred_element_type=F32,
            )
        total[which, :, halves[h]] = value
        part[which, :, halves[h]] = value.astype(BF16)
        to_all_terms(
            lambda j: remote(
                part.at[which, row_block((t + j) % nterm), halves[h]],
                arrived.at[which, nterm - 1 - j, :, halves[h]],
                part_send.at[which, h],
                part_recv.at[which, h],
                on_term(j),
            )
        )

    def reduce(which, h):
        wait_for(arrived.at[which, other_t, :, halves[h]], part_recv.at[which, h])
        value = total[which, my_rows, halves[h]]
        for j in range(nterm - 1):
            value = value + arrived[which, j, :, halves[h]].astype(F32)
        sums[which, :, halves[h]] = value.astype(BF16)
        remote(
            sums.at[which, :, halves[h]],
            sums_p.at[which, :, halves[h]],
            swap_send.at[which, h],
            swap_recv.at[which, h],
            partner,
        ).start()

    def swapped(which, h):
        wait_for(sums_p.at[which, :, halves[h]], swap_recv.at[which, h])

    def contribution(d, h):
        sector = ((z + nz - d) % nz) * 2 + c
        value = jnp.zeros((rows, wide), F32)
        for which in range(2):
            mine = jnp.where(ends[1 - which] == sector, 1.0, 0.0).astype(F32)
            value = value + sums[which, :, halves[h]].astype(F32) * mine
            theirs = tag_row(1 - which) == sector.astype(F32)
            value = value + jnp.where(theirs, sums_p[which, :, halves[h]].astype(F32), 0.0)
        return value.astype(BF16)

    def scatter(h):
        for d in far_first:
            leaving[d, :, halves[h]] = contribution(d, h)
            remote(
                leaving.at[d, :, halves[h]],
                landed.at[d, :, halves[h]],
                land_send.at[h],
                land_recv.at[h],
                on_z(d),
            ).start()

    keep = []

    def finish(h):
        value = contribution(0, h).astype(F32)
        wait_for(landed.at[other_z, :, halves[h]], land_recv.at[h])
        for d in range(1, nz):
            value = value + landed[d, :, halves[h]].astype(F32)
        mine_v[:, halves[h]] = value.astype(BF16)
        to_all_terms(
            lambda j: remote(
                mine_v.at[:, halves[h]],
                out.at[0, my_rows, halves[h]],
                out_send.at[h],
                out_recv.at[h],
                on_term(j),
            )
        )
        keep.append(
            pltpu.make_async_copy(
                mine_v.at[:, halves[h]], out.at[0, my_rows, halves[h]], local_sem.at[2 + h]
            )
        )
        keep[-1].start()

    load_left.wait()
    inner(0)
    load_right.wait()
    outer(0, 0)
    outer(0, 1)
    inner(1)
    reduce(0, 0)
    outer(1, 0)
    reduce(0, 1)
    outer(1, 1)
    swapped(0, 0)
    swapped(0, 1)
    reduce(1, 0)
    swapped(1, 0)
    scatter(0)
    reduce(1, 1)
    swapped(1, 1)
    scatter(1)
    finish(0)
    finish(1)

    wait_for(label, hand_send.at[4])
    for h in range(2):
        wait_for(column[h].at[other_z], column_send.at[h])
        wait_for(landed.at[other_z, :, halves[h]], land_send.at[h])
        for which in range(2):
            wait_for(given.at[which, :, halves[h]], hand_send.at[2 * which + h])
            wait_for(blocks.at[which, other_rows, halves[h]], block_send.at[which, h])
            wait_for(part.at[which, other_rows, halves[h]], part_send.at[which, h])
            wait_for(sums.at[which, :, halves[h]], swap_send.at[which, h])
        keep[h].wait()
        wait_for(out.at[0, other_rows, halves[h]], out_send.at[h])
        wait_for(out.at[0, other_rows, halves[h]], out_recv.at[h])


def solution(mesh):
    nsec, nterm = mesh.shape["sec"], mesh.shape["term"]
    placed = (
        P("sec", None, None),
        P("sec", "term", None, None),
        P("sec", "term", None, None),
        P("sec", "term"),
        P("sec"),
        P("sec"),
    )

    def local(psi, left_ops, right_ops, term_mask, pair_src, pair_dst):
        order, terms = psi.shape[1], left_ops.shape[1]
        rows, nz = order // nterm, nsec // 2
        anywhere = pl.BlockSpec(memory_space=pl.ANY)
        dma = pltpu.SemaphoreType.DMA
        return pl.pallas_call(
            functools.partial(kernel, (nsec, nterm, terms, order)),
            out_shape=jax.ShapeDtypeStruct(psi.shape, BF16),
            in_specs=[anywhere] * 6,
            out_specs=anywhere,
            scratch_shapes=[
                pltpu.VMEM((terms, order, order), BF16),
                pltpu.VMEM((terms, order, order), BF16),
                pltpu.VMEM((nz, rows, order // 2), BF16),
                pltpu.VMEM((nz, rows, order // 2), BF16),
                pltpu.VMEM((2, rows, order), BF16),
                pltpu.VMEM((2, rows, order), BF16),
                pltpu.VMEM((2, order, order), BF16),
                pltpu.VMEM((16, 128), F32),
                pltpu.VMEM((16, 128), F32),
                pltpu.VMEM((terms, order, order), BF16),
                pltpu.VMEM((2, order, order), F32),
                pltpu.VMEM((2, order, order), BF16),
                pltpu.VMEM((2, nterm, rows, order), BF16),
                pltpu.VMEM((2, rows, order), BF16),
                pltpu.VMEM((2, rows, order), BF16),
                pltpu.VMEM((nz, rows, order), BF16),
                pltpu.VMEM((nz, rows, order), BF16),
                pltpu.VMEM((rows, order), BF16),
                pltpu.SMEM((1, terms), jnp.int32),
                pltpu.SMEM((1,), jnp.int32),
                pltpu.SMEM((1,), jnp.int32),
                dma((6,)),
                dma((5,)),
                dma((5,)),
                dma((2,)),
                dma((2,)),
                dma((2, 2)),
                dma((2, 2)),
                dma((2, 2)),
                dma((2, 2)),
                dma((2, 2)),
                dma((2, 2)),
                dma((2,)),
                dma((2,)),
                dma((2,)),
                dma((2,)),
            ],
            compiler_params=pltpu.CompilerParams(
                collective_id=0, has_side_effects=True, vmem_limit_bytes=67043328
            ),
        )(psi, left_ops, right_ops, term_mask, pair_src, pair_dst)

    return jax.shard_map(
        local, mesh=mesh, in_specs=placed, out_specs=P("sec", None, None), check_vma=False
    )
```

time: 72.6 us -> 65.5 us (0.902)
  Pallas kernels: 66.7 us -> 62.1 us
  local copies, waits for them, and re-layouts: 4.37 us -> 1.87 us
    pallas_call x1, Pallas kernels: 66.7 us -> 62.1 us  [local(): pl.pallas_call(functools.partial(kernel, (nsec, nterm, terms, order)), ou...]
    unnamed x7 -> x1, local copies, waits for them, and re-layouts: 4.37 us -> 1.87 us
where the time goes in v2:
time: 65.5 us; the launch traced here: 65.3 us
  Pallas kernels  62.1 us (95%)
  local copies, waits for them, and re-layouts  1.87 us (3%)
  between operations  1.3 us (2%)
    pallas_call x1, Pallas kernels, local(): pl.pallas_call(functools.partial(kernel, (nsec, nterm, terms, order)), ou...  62.1 us
    unnamed x1, local copies, waits for them, and re-layouts  1.87 us

profile of v2, /device:TPU:1, one launch (start us, length us, event | category | flops | bytes accessed | tf_op | source)
XLA Modules:
  0.0 65.3 jit_solution(3554825637012377298)
XLA Ops:
  1.3 62.1 %shard_map.64 = bf16[1,512,512]{2,1,0:T(8,128)(2,1)} custom-call(bf16[1,512,512]{2,1,0:T(8,128)(2,1)} %psi.1, bf16[1,6,512,512]{3,2,1,0:T(8,128)(2,1)} %left.1, bf16[1,6,512,512]{3,2,1,0:T(8,128)(2,1)} %right.1, s32[1,6]{1,0:T(1,128)} %mask.1, s32[1]{0:T(128)S(6)} %copy.8.src, s32[1]{0:T(128)S(6)} %copy.9.dst), custom_call_target="tpu_custom_call" | custom-call | tf_op jit(solution)/shard_map/pallas_call | solution.py:354
  63.4 1.9 %copy.10 = bf16[1,512,512]{2,1,0:T(8,128)(2,1)} copy(bf16[1,512,512]{2,1,0:T(8,128)(2,1)} %shard_map.64) | data formatting | bytes 1048576

commit v3 on v2

--- a/solution.py
+++ b/solution.py
@@ -136,8 +136,13 @@
         copy.wait()
     pl.semaphore_wait(barrier, nz + nterm - 1)
 
+    load_left = pltpu.make_async_copy(left.at[0], left_v, local_sem.at[0])
+    load_right = pltpu.make_async_copy(right.at[0], right_v, local_sem.at[1])
+
     remote(label, label_p, hand_send.at[4], hand_recv.at[4], partner).start()
     for h in range(2):
+        if h == 1:
+            wait_for(column[0].at[other_z], column_send.at[0])
         for d in far_first:
             remote(
                 column[h].at[0],
@@ -146,10 +151,9 @@
                 column_recv.at[h],
                 on_z(d),
             ).start()
-    load_left = pltpu.make_async_copy(left.at[0], left_v, local_sem.at[0])
-    load_right = pltpu.make_async_copy(right.at[0], right_v, local_sem.at[1])
-    load_left.start()
-    load_right.start()
+        if h == 0:
+            load_left.start()
+            load_right.start()
 
     def tag_row(which):
         row = label_p[8 * which : 8 * which + 1, :]
@@ -196,6 +200,7 @@
     place(0, 0)
     give(1)
     place(0, 1)
+    wait_for(blocks.at[0, other_rows, halves[1]], block_send.at[0, 1])
     place(1, 0)
     place(1, 1)
 
@@ -323,11 +328,13 @@
 
     wait_for(label, hand_send.at[4])
     for h in range(2):
-        wait_for(column[h].at[other_z], column_send.at[h])
+        if h == 1:
+            wait_for(column[h].at[other_z], column_send.at[h])
         wait_for(landed.at[other_z, :, halves[h]], land_send.at[h])
         for which in range(2):
             wait_for(given.at[which, :, halves[h]], hand_send.at[2 * which + h])
-            wait_for(blocks.at[which, other_rows, halves[h]], block_send.at[which, h])
+            if (which, h) != (0, 1):
+                wait_for(blocks.at[which, other_rows, halves[h]], block_send.at[which, h])
             wait_for(part.at[which, other_rows, halves[h]], part_send.at[which, h])
             wait_for(sums.at[which, :, halves[h]], swap_send.at[which, h])
         keep[h].wait()

time: 65.5 us -> 63 us (0.962)
  Pallas kernels: 62.1 us -> 59.7 us
    pallas_call x1, Pallas kernels: 62.1 us -> 59.7 us  [local(): pl.pallas_call(functools.partial(kernel, (nsec, nterm, terms, order)), ou...]
where the time goes in v3:
time: 63 us; the launch traced here: 62.8 us
  Pallas kernels  59.7 us (95%)
  local copies, waits for them, and re-layouts  1.87 us (3%)
  between operations  1.3 us (2%)
    pallas_call x1, Pallas kernels, local(): pl.pallas_call(functools.partial(kernel, (nsec, nterm, terms, order)), ou...  59.7 us
    unnamed x1, local copies, waits for them, and re-layouts  1.87 us

profile of v3, /device:TPU:1, one launch (start us, length us, event | category | flops | bytes accessed | tf_op | source)
XLA Modules:
  0.0 62.8 jit_solution(11812732976062236700)
XLA Ops:
  1.3 59.7 %shard_map.64 = bf16[1,512,512]{2,1,0:T(8,128)(2,1)} custom-call(bf16[1,512,512]{2,1,0:T(8,128)(2,1)} %psi.1, bf16[1,6,512,512]{3,2,1,0:T(8,128)(2,1)} %left.1, bf16[1,6,512,512]{3,2,1,0:T(8,128)(2,1)} %right.1, s32[1,6]{1,0:T(1,128)} %mask.1, s32[1]{0:T(128)S(6)} %copy.8.src, s32[1]{0:T(128)S(6)} %copy.9.dst), custom_call_target="tpu_custom_call" | custom-call | tf_op jit(solution)/shard_map/pallas_call | solution.py:361
  61.0 1.9 %copy.10 = bf16[1,512,512]{2,1,0:T(8,128)(2,1)} copy(bf16[1,512,512]{2,1,0:T(8,128)(2,1)} %shard_map.64) | data formatting | bytes 1048576

commit v4 on v3

--- a/solution.py
+++ b/solution.py
@@ -311,10 +311,10 @@
     outer(0, 0)
     outer(0, 1)
     inner(1)
+    outer(1, 0)
+    outer(1, 1)
     reduce(0, 0)
-    outer(1, 0)
     reduce(0, 1)
-    outer(1, 1)
     swapped(0, 0)
     swapped(0, 1)
     reduce(1, 0)

time: 63 us -> 62 us (0.984)
  Pallas kernels: 59.7 us -> 58.7 us
    pallas_call x1, Pallas kernels: 59.7 us -> 58.7 us  [local(): pl.pallas_call(functools.partial(kernel, (nsec, nterm, terms, order)), ou...]
where the time goes in v4:
time: 62 us; the launch traced here: 61.8 us
  Pallas kernels  58.7 us (95%)
  local copies, waits for them, and re-layouts  1.87 us (3%)
  between operations  1.3 us (2%)
    pallas_call x1, Pallas kernels, local(): pl.pallas_call(functools.partial(kernel, (nsec, nterm, terms, order)), ou...  58.7 us
    unnamed x1, local copies, waits for them, and re-layouts  1.87 us

profile of v4, /device:TPU:1, one launch (start us, length us, event | category | flops | bytes accessed | tf_op | source)
XLA Modules:
  0.0 61.8 jit_solution(8994367077916958318)
XLA Ops:
  1.3 58.7 %shard_map.64 = bf16[1,512,512]{2,1,0:T(8,128)(2,1)} custom-call(bf16[1,512,512]{2,1,0:T(8,128)(2,1)} %psi.1, bf16[1,6,512,512]{3,2,1,0:T(8,128)(2,1)} %left.1, bf16[1,6,512,512]{3,2,1,0:T(8,128)(2,1)} %right.1, s32[1,6]{1,0:T(1,128)} %mask.1, s32[1]{0:T(128)S(6)} %copy.8.src, s32[1]{0:T(128)S(6)} %copy.9.dst), custom_call_target="tpu_custom_call" | custom-call | tf_op jit(solution)/shard_map/pallas_call | solution.py:361
  60.0 1.9 %copy.10 = bf16[1,512,512]{2,1,0:T(8,128)(2,1)} copy(bf16[1,512,512]{2,1,0:T(8,128)(2,1)} %shard_map.64) | data formatting | bytes 1048576

commit v5 on v4

--- a/solution.py
+++ b/solution.py
@@ -200,7 +200,7 @@
     place(0, 0)
     give(1)
     place(0, 1)
-    wait_for(blocks.at[0, other_rows, halves[1]], block_send.at[0, 1])
+    wait_for(blocks.at[0, other_rows, halves[0]], block_send.at[0, 0])
     place(1, 0)
     place(1, 1)
 
@@ -333,7 +333,7 @@
         wait_for(landed.at[other_z, :, halves[h]], land_send.at[h])
         for which in range(2):
             wait_for(given.at[which, :, halves[h]], hand_send.at[2 * which + h])
-            if (which, h) != (0, 1):
+            if (which, h) != (0, 0):
                 wait_for(blocks.at[which, other_rows, halves[h]], block_send.at[which, h])
             wait_for(part.at[which, other_rows, halves[h]], part_send.at[which, h])
             wait_for(sums.at[which, :, halves[h]], swap_send.at[which, h])

time: 62 us -> 62.6 us (level)
  no operation moved by 1% of the time
where the time goes in v5:
time: 62.6 us; the launch traced here: 62.4 us
  Pallas kernels  59.2 us (95%)
  local copies, waits for them, and re-layouts  1.87 us (3%)
  between operations  1.3 us (2%)
    pallas_call x1, Pallas kernels, local(): pl.pallas_call(functools.partial(kernel, (nsec, nterm, terms, order)), ou...  59.2 us
    unnamed x1, local copies, waits for them, and re-layouts  1.87 us

profile of v5, /device:TPU:1, one launch (start us, length us, event | category | flops | bytes accessed | tf_op | source)
XLA Modules:
  0.0 62.4 jit_solution(8242634121587158883)
XLA Ops:
  1.3 59.2 %shard_map.64 = bf16[1,512,512]{2,1,0:T(8,128)(2,1)} custom-call(bf16[1,512,512]{2,1,0:T(8,128)(2,1)} %psi.1, bf16[1,6,512,512]{3,2,1,0:T(8,128)(2,1)} %left.1, bf16[1,6,512,512]{3,2,1,0:T(8,128)(2,1)} %right.1, s32[1,6]{1,0:T(1,128)} %mask.1, s32[1]{0:T(128)S(6)} %copy.8.src, s32[1]{0:T(128)S(6)} %copy.9.dst), custom_call_target="tpu_custom_call" | custom-call | tf_op jit(solution)/shard_map/pallas_call | solution.py:361
  60.5 1.9 %copy.10 = bf16[1,512,512]{2,1,0:T(8,128)(2,1)} copy(bf16[1,512,512]{2,1,0:T(8,128)(2,1)} %shard_map.64) | data formatting | bytes 1048576
